TPU v7x, 256 devices: a whole 4x4x8 slice. The times are simulated.
256 devices in a mesh: dp: 4 (over x), table: 64 (over y, z, core).
Axes of the slice: x: 4, y: 4, z: 8, core: 2. Of those that a mesh axis runs over, the one named last changes fastest.
Arguments:
- shard_of: int32 [2048, 200, 3], P(('dp', 'table')), may hold values from 0 to 63, all different within a row; in each aligned block of 1600 rows (0 to 1599, 1600 to 3199, ..., all dimensions but the last counted through in order) at most 152 rows name the same one
- offsets: int32 [2048, 200, 3], P(('dp', 'table')), may hold values from 0 to 2047
- table: bfloat16 [3, 131072, 256], P(None, 'table'), may hold values from -4 to 4
- weight_one: bfloat16 [768, 256], replicated, may hold values from -0.21875 to 0.21875
- gain_one: float32 [256], replicated, may hold values from 0.5 to 1.5
- weight_two: bfloat16 [768, 256], replicated, may hold values from -0.21875 to 0.21875
- gain_two: float32 [256], replicated, may hold values from 0.5 to 1.5
- grad_out: bfloat16 [2048, 200, 256], P(('dp', 'table')), may hold values from -6 to 6
Outputs:
- block_out: bfloat16 [2048, 200, 256], P(('dp', 'table'))
- grad_weight_one: float32 [768, 256], replicated
- grad_weight_two: float32 [768, 256], replicated
- grad_gain_one: float32 [256], replicated
- grad_gain_two: float32 [256], replicated
- table_grad: float32 [3, 131072, 256], P(None, 'table', 'dp')
Inputs may be any that keep to these rules, and one draw needn't show every extreme that they name: `shard_of`: the three lookups of one item go to three different shards; at most 152 lookups of the items of one device go to one shard, and exactly 152 for some shard of some device.
All inputs are finite; a program needn't handle non-finite values.
Results may differ from a plain program's by a relative error of at most 0.017.
Values may be sent and summed in bfloat16 or wider, within the bound.
A program may use at most 128 MiB of HBM per device.

v0:
```python
import math
import jax
import jax.numpy as jnp
from jax import lax
from jax.sharding import PartitionSpec as P

GELU_C = 0.7978845608028654
GELU_K = 0.044715


def shifted(values, spacing):
    return jnp.pad(values, ((0, 0), (spacing, 0), (0, 0)))[:, : values.shape[1], :]


def unshifted(values, spacing):
    return jnp.pad(values, ((0, 0), (0, spacing), (0, 0)))[:, spacing:, :]


def stack_taps(values, spacing):
    return jnp.concatenate(
        [values, shifted(values, spacing), shifted(values, 2 * spacing)], axis=-1
    )


def gelu_parts(inputs):
    inner = GELU_C * (inputs + GELU_K * inputs * inputs * inputs)
    tangent = jnp.tanh(inner)
    output = 0.5 * inputs * (1.0 + tangent)
    slope = 0.5 * (1.0 + tangent) + 0.5 * inputs * (1.0 - tangent * tangent) * GELU_C * (
        1.0 + 3.0 * GELU_K * inputs * inputs
    )
    return (output, slope)


def layer_forward(values, weight, gain, spacing):
    sessions, length, width = values.shape
    stacked = stack_taps(values, spacing).reshape(sessions * length, 3 * width)
    before_norm = jnp.dot(stacked, weight, preferred_element_type=jnp.float32)
    centred = before_norm - jnp.mean(before_norm, axis=-1, keepdims=True)
    inv_std = lax.rsqrt(jnp.mean(centred * centred, axis=-1, keepdims=True) + 1e-05)
    normal = centred * inv_std
    output, slope = gelu_parts(normal * gain)
    return (output, (stacked, normal, inv_std, slope))


def layer_backward(grad_output, weight, gain, saved, spacing, sessions, length):
    stacked, normal, inv_std, slope = saved
    width = weight.shape[1]
    grad_scaled = grad_output * slope
    grad_gain = jnp.sum(grad_scaled * normal, axis=0)
    grad_normal = grad_scaled * gain
    grad_before = inv_std * (
        grad_normal
        - jnp.mean(grad_normal, axis=-1, keepdims=True)
        - normal * jnp.mean(grad_normal * normal, axis=-1, keepdims=True)
    )
    grad_before = grad_before.astype(jnp.bfloat16)
    grad_weight = lax.dot_general(
        stacked, grad_before, (((0,), (0,)), ((), ())), preferred_element_type=jnp.float32
    )
    grad_taps = lax.dot_general(
        grad_before, weight, (((1,), (1,)), ((), ())), preferred_element_type=jnp.float32
    ).reshape(sessions, length, 3 * width)
    grad_input = (
        grad_taps[..., :width]
        + unshifted(grad_taps[..., width : 2 * width], spacing)
        + unshifted(grad_taps[..., 2 * width :], 2 * spacing)
    )
    return (grad_input, grad_weight, grad_gain)


def to_owners(grad_rows, slot_place, shards, slot_count, width):
    outgoing = (
        jnp.zeros((shards * slot_count, width), jnp.bfloat16)
        .at[slot_place]
        .set(grad_rows)
        .reshape(shards, slot_count, width)
    )
    return lax.all_to_all(outgoing, "table", split_axis=0, concat_axis=0, tiled=True)


def on_device(shard_of, offsets, table, weight_one, gain_one, weight_two, gain_two, grad_out):
    sessions, length, _ = shard_of.shape
    width = table.shape[2]
    rows_dev = table.shape[1]
    item_count = sessions * length
    shards = lax.axis_size("table")
    groups = lax.axis_size("dp")
    quarter = width // groups
    slot_count = 8 * ((6 * item_count + 8 * shards - 1) // (8 * shards))
    target = shard_of.reshape(-1)
    table_pick = jnp.tile(jnp.arange(3, dtype=jnp.int32), item_count)
    row_codes = table_pick * rows_dev + offsets.reshape(-1)
    onehot = (jnp.arange(shards, dtype=jnp.int32)[:, None] == target[None, :]).astype(jnp.int32)
    before = jnp.cumsum(onehot, axis=1) - onehot
    slot_rank = jnp.sum(before * onehot, axis=0)
    slot_place = target * slot_count + slot_rank
    requests = (
        jnp.full((shards * slot_count,), -1, jnp.int32)
        .at[slot_place]
        .set(row_codes)
        .reshape(shards, slot_count)
    )
    table_flat = table.reshape(3 * rows_dev, width)
    asked_rows = lax.all_to_all(requests, "table", split_axis=0, concat_axis=0, tiled=True)
    found_rows = jnp.take(table_flat, jnp.maximum(asked_rows, 0), axis=0)
    found_rows = jnp.where((asked_rows >= 0)[..., None], found_rows, jnp.zeros((), jnp.bfloat16))
    sent_back = lax.all_to_all(found_rows, "table", split_axis=0, concat_axis=0, tiled=True)
    picked = jnp.take(sent_back.reshape(shards * slot_count, width), slot_place, axis=0).reshape(
        item_count, 3, width
    )
    embedded = (
        jnp.sum(picked.astype(jnp.float32), axis=1)
        .astype(jnp.bfloat16)
        .reshape(sessions, length, width)
    )
    act_one, saved_one = layer_forward(embedded, weight_one, gain_one, 1)
    hidden = act_one.astype(jnp.bfloat16).reshape(sessions, length, width)
    act_two, saved_two = layer_forward(hidden, weight_two, gain_two, 2)
    block_out = (
        (embedded.reshape(item_count, width).astype(jnp.float32) + act_two)
        .astype(jnp.bfloat16)
        .reshape(sessions, length, width)
    )
    grad_top = grad_out.reshape(item_count, width).astype(jnp.float32)
    scale = 1.0 / math.sqrt(item_count * groups * shards)
    grad_hidden, second_weights, second_gains = layer_backward(
        grad_top, weight_two, gain_two, saved_two, 2, sessions, length
    )
    grad_inner, first_weights, first_gains = layer_backward(
        grad_hidden.reshape(item_count, width), weight_one, gain_one, saved_one, 1, sessions, length
    )
    grad_embed = (grad_top + grad_inner.reshape(item_count, width)).astype(jnp.bfloat16)
    repeated = jnp.repeat(grad_embed, 3, axis=0)
    arrived = to_owners(repeated, slot_place, shards, slot_count, width)
    dense_grad = (
        jnp.zeros((3 * rows_dev, width), jnp.float32)
        .at[jnp.maximum(asked_rows, 0).reshape(-1)]
        .add(arrived.reshape(-1, width).astype(jnp.float32))
    )
    table_grad = lax.psum_scatter(
        dense_grad.astype(jnp.bfloat16), "dp", scatter_dimension=1, tiled=True
    ).astype(jnp.float32)
    table_grad = table_grad.reshape(3, rows_dev, quarter)
    totals = lax.psum((first_weights, second_weights, first_gains, second_gains), ("dp", "table"))
    return (
        block_out,
        totals[0] * scale,
        totals[1] * scale,
        totals[2] * scale,
        totals[3] * scale,
        table_grad,
    )


def solution(mesh):
    placed = (
        P(("dp", "table"), None, None),
        P(("dp", "table"), None, None),
        P(None, "table", None),
        P(),
        P(),
        P(),
        P(),
        P(("dp", "table"), None, None),
    )
    return jax.shard_map(
        on_device,
        mesh=mesh,
        in_specs=placed,
        out_specs=(P(("dp", "table"), None, None), P(), P(), P(), P(), P(None, "table", "dp")),
        check_vma=False,
    )
```

profile of v0, /device:TPU:2, one launch (start us, length us, event | category | flops | bytes accessed | tf_op | source)
XLA Modules:
  0.0 678.1 jit_solution(2011394004684885150)
XLA Ops:
  8.9 2.0 copy.48
  10.9 0.9 iota_multiply_fusion
  11.9 1.2 copy.53
  13.1 1.7 mul.226
  14.8 1.2 copy.54
  16.0 1.6 reshape.223
  17.7 1.6 reshape.220
  19.3 1.6 mul.229
  21.0 1.1 pad.33
  22.1 2.4 reshape.221
  24.6 35.5 %reduce-window.6 = s32[64,38,128]{2,1,0:T(8,128)} reduce-window(s32[64,38,128]{2,1,0:T(8,128)} %reshape.221, s32[]{:T(128)} %constant.37.clone.1), window={size=1x1x128 pad=0_0x0_0x127_0}, to_apply=%region_0.0 | reduce-window | flops 39534592 | bytes 2490372 | tf_op jit(solution)/shard_map/reduce-window
  60.1 2.8 slice.72
  62.8 1.9 copy.59
  64.9 1.6 broadcast_add_fusion
  67.1 22.8 %scatter_custom_fusion = s32[9728]{0:T(1024)S(1)} fusion(s32[4800]{0:T(1024)S(1)} %fusion.30, s32[4800]{0:T(1024)S(1)} %add.145, s32[]{:T(128)} %constant.40.clone.1), kind=kCustom, calls=%fused_computation.82 | custom fusion | bytes 38916 | tf_op jit(solution)/shard_map/scatter | solution.py:101
  90.1 21.6 %all_to_all.19 = s32[64,1,152]{2,1,0:T(1,128)S(1)} all-to-all(s32[64,1,152]{2,1,0:T(1,128)S(1)} %all_to_all.12), channel_id=1, replica_groups=mesh['dp'=4,'table'=64] {'table'}, dimensions={0} | all-to-all | bytes 77824 | tf_op jit(solution)/shard_map/all_to_all | solution.py:105
  111.8 27.6 %gather_fusion = bf16[9728,256]{1,0:T(8,128)(2,1)} fusion(bf16[6144,256]{1,0:T(8,128)(2,1)S(1)} %bitcast.55, s32[10240]{0:T(1024)S(1)} %pad_clamp_fusion), kind=kCustom, calls=%fused_computation | custom fusion | bytes 10000384 | tf_op jit(solution)/shard_map/jit(_take)/gather | solution.py:106
  139.5 8.1 %select_select_fusion = bf16[64,152,256]{2,1,0:T(8,128)(2,1)} fusion(bf16[64,152,256]{2,1,0:T(8,128)(2,1)} %bitcast.61, pred[64,152]{1,0:T(8,128)(4,1)S(1)} %get-tuple-element.57, pred[64,152]{1,0:T(8,128)(4,1)S(1)} %get-tuple-element.56), kind=kLoop, calls=%fused_computation.7 | loop fusion | flops 4980736 | bytes 9980928 | tf_op jit(solution)/shard_map/jit(_where)/select_n | solution.py:107
  147.6 6.2 all-to-all-start.1
  155.3 110.9 %all-to-all-done.1 = bf16[64,152,256]{2,1,0:T(8,128)(2,1)} async-done(((bf16[64,152,256]{2,1,0:T(8,128)(2,1)}), bf16[64,152,256]{2,1,0:T(8,128)(2,1)}, u32[]{:S(2)}, u32[]{:S(2)}) %all-to-all-start.1) | async-done | bytes 4980768 | tf_op jit(solution)/shard_map/all_to_all | solution.py:108
  266.2 13.8 %gather_fusion.1 = bf16[4800,256]{1,0:T(8,128)(2,1)S(1)} fusion(bf16[9728,256]{1,0:T(8,128)(2,1)} %bitcast.6, s32[5120]{0:T(1024)S(1)} %pad_clamp_fusion.1), kind=kCustom, calls=%fused_computation.1 | custom fusion | bytes 4934400 | tf_op jit(solution)/shard_map/jit(_take)/gather | solution.py:109
  280.0 3.8 gather.12
  283.8 13.2 %select_reduce_fusion = bf16[1600,256]{1,0:T(8,128)(2,1)S(1)} fusion(bf16[1600,3,256]{2,1,0:T(4,128)(2,1)} %gather.12, pred[1600,3]{1,0:T(8,128)(4,1)S(1)} %copy.52), kind=kLoop, calls=%fused_computation.8 | loop fusion | flops 2048000 | bytes 3281600 | tf_op jit(solution)/shard_map/reduce_sum | solution.py:113
  298.0 0.9 fusion.37
  299.6 1.1 multiply_convert_fusion.2
  302.1 0.9 fusion.38
  304.1 1.5 convert_multiply_fusion
  305.7 1.0 multiply_reduce_fusion
  306.7 2.4 multiply_convert_fusion.1
  310.6 1.7 fusion.20
  312.3 1.0 multiply_reduce_fusion.1
  313.3 1.3 multiply_convert_fusion
  316.3 7.5 %broadcast_in_dim.70 = bf16[1600,3,256]{2,1,0:T(4,128)(2,1)} broadcast(bf16[1600,256]{1,0:T(8,128)(2,1)S(1)} %fusion.9), dimensions={0,2} | broadcast | bytes 3276800 | tf_op jit(solution)/shard_map/broadcast_in_dim | solution.py:134
  323.8 7.2 %reshape.269 = bf16[4800,256]{1,0:T(8,128)(2,1)} reshape(bf16[1600,3,256]{2,1,0:T(4,128)(2,1)} %broadcast_in_dim.70) | data formatting | bytes 4915200 | tf_op jit(solution)/shard_map/reshape | solution.py:134
  331.0 28.4 %scatter_custom_fusion.1 = bf16[9728,256]{1,0:T(8,128)(2,1)} fusion(s32[4800]{0:T(1024)S(1)} %fusion.30, bf16[4800,256]{1,0:T(8,128)(2,1)} %reshape.269, bf16[]{:T(256)} %constant.72.clone.1), kind=kCustom, calls=%fused_computation.10 | custom fusion | bytes 4981248 | tf_op jit(solution)/shard_map/scatter | solution.py:76
  359.5 6.4 all-to-all-start.2
  366.0 3.6 fusion.24
  369.6 1.8 fusion.26
  371.4 111.0 %all-to-all-done.2 = bf16[64,152,256]{2,1,0:T(8,128)(2,1)} async-done(((bf16[64,152,256]{2,1,0:T(8,128)(2,1)}), bf16[64,152,256]{2,1,0:T(8,128)(2,1)}, u32[]{:S(2)}, u32[]{:S(2)}) %all-to-all-start.2) | async-done | bytes 4980768 | tf_op jit(solution)/shard_map/all_to_all | solution.py:79
  482.4 64.7 %scatter_custom_fusion.2 = f32[6144,256]{1,0:T(8,128)} fusion(s32[9728]{0:T(1024)S(1)} %reshape.243, bf16[9728,256]{1,0:T(8,128)(2,1)} %bitcast.24, f32[]{:T(128)} %constant.73.clone.1), kind=kCustom, calls=%fused_computation.5 | custom fusion | flops 4980736 | bytes 11272196 | tf_op jit(solution)/shard_map/scatter-add | solution.py:139
  547.1 3.1 convert_element_type.64
  550.2 3.1 copy.60
  553.4 76.3 %all-reduce.9 = (f32[256]{0:T(256)S(1)}, f32[256]{0:T(256)S(1)}) all-reduce(f32[256]{0:T(256)S(1)} %get-tuple-element.38, f32[256]{0:T(256)S(1)} %get-tuple-element.36), channel_id=1, replica_groups=mesh['dp'=4,'table'=64] {'dp','table'}, use_global_device_ids=true, to_apply=%region_16.17 | all-reduce | flops 512 | bytes 4096 | tf_op jit(solution)/shard_map/psum | solution.py:145
  630.8 33.9 %all-reduce.13.cloned.1.call-done = (f32[768,256]{1,0:T(8,128)}, f32[768,256]{1,0:T(8,128)}) async-done(((f32[768,256]{1,0:T(8,128)}, f32[768,256]{1,0:T(8,128)}), (f32[768,256]{1,0:T(8,128)}, f32[768,256]{1,0:T(8,128)})) %all-reduce.13.cloned.1.call-update) | async-done | bytes 1572880 | tf_op jit(solution)/shard_map/psum | solution.py:145
  664.7 2.2 broadcast_multiply_fusion.1
  666.9 1.0 broadcast_multiply_fusion
  667.8 1.4 bitcast_convert_fusion
  669.2 1.2 copy.70
  (83 shorter events, 12.1 us)
Async XLA Ops:
  8.0 103.8 %copy-start = (bf16[3,2048,256]{2,1,0:T(8,128)(2,1)S(1)}, bf16[3,2048,256]{2,1,0:T(8,128)(2,1)}, u32[]{:S(2)}) copy-start(bf16[3,2048,256]{2,1,0:T(8,128)(2,1)} %param.10) | copy-start | bytes 9437188
  8.9 5.9 copy-start.17
  147.6 118.6 %all-to-all-start.1 = ((bf16[64,152,256]{2,1,0:T(8,128)(2,1)}), bf16[64,152,256]{2,1,0:T(8,128)(2,1)}, u32[]{:S(2)}, u32[]{:S(2)}) async-start(bf16[64,152,256]{2,1,0:T(8,128)(2,1)} %select_select_fusion), calls=%async_computation.1 | async-start | bytes 9961472 | tf_op jit(solution)/shard_map/all_to_all | solution.py:108
  297.0 1.0 copy-start.16
  297.4 1.6 copy-start.8
  297.4 1.6 copy-start.10
  299.0 0.7 copy-start.18
  300.8 2.2 copy-start.6
  300.8 1.3 copy-start.15
  301.2 1.8 copy-start.12
  301.2 1.8 copy-start.13
  303.0 1.1 copy-start.7
  303.0 1.1 copy-start.19
  309.1 0.9 copy-start.2
  314.6 0.9 copy-start.4
  359.5 6.5 copy-start.3
  359.5 122.9 %all-to-all-start.2 = ((bf16[64,152,256]{2,1,0:T(8,128)(2,1)}), bf16[64,152,256]{2,1,0:T(8,128)(2,1)}, u32[]{:S(2)}, u32[]{:S(2)}) async-start(bf16[64,152,256]{2,1,0:T(8,128)(2,1)} %bitcast.60), calls=%async_computation.2 | async-start | bytes 9961472 | tf_op jit(solution)/shard_map/all_to_all | solution.py:79
  365.9 3.7 copy-start.5
  365.9 298.8 %all-reduce.13.cloned.1.call-start = ((), (), s32[]{:S(2)}) async-start(), calls=%async_computation.5 | async-start | bytes 3145728 | tf_op jit(solution)/shard_map/psum | solution.py:145
  365.9 3.6 copy-start.9
  365.9 3.6 copy-start.11
  371.4 296.4 %reduce-scatter.4.cloned.1.call-start = ((), (), s32[]{:S(2)}) async-start(), calls=%async_computation.4 | async-start | bytes 3932160
  664.7 2.2 copy-start.14
  667.8 2.6 copy-start.1
Sparse Core Ops, SparseCore 0:
  372.8 291.8 all-reduce.12
Sparse Core Ops, SparseCore 1:
  553.5 37.5 reduce-scatter.3
where the time goes:
time: 690 us; the launch traced here: 678 us
  waiting for transfers between devices  256 us (37%)
  other arithmetic  146 us (21%)
  local copies, waits for them, and re-layouts  140 us (20%)
  blocking collectives  97.9 us (14%)
  between operations  16.2 us (2%)
  starting transfers between devices  12.6 us (2%)
  matrix products  8.91 us (1%)
    all_to_all x1, waiting for transfers between devices, to_owners(): lax.all_to_all(outgoing, 'table', split_axis=0, concat_axis=0, tiled=True)  111 us
    all_to_all x1, waiting for transfers between devices, on_device(): lax.all_to_all(found_rows, 'table', split_axis=0, concat_axis=0, tiled=True)  111 us
    psum x1, blocking collectives, on_device(): lax.psum((first_weights, second_weights, first_gains, second_gains), ('dp...  76.3 us
    scatter-add x1, other arithmetic, on_device(): dense_grad = jnp.zeros((3 * rows_dev, width), jnp.float32).at[jnp.maximum...  64.7 us
    another operation x3, other arithmetic  37.3 us
    psum x1, waiting for transfers between devices, on_device(): lax.psum((first_weights, second_weights, first_gains, second_gains), ('dp...  33.9 us
    scatter x1, local copies, waits for them, and re-layouts, to_owners(): outgoing = jnp.zeros((shards * slot_count, width), jnp.bfloat16).at[slot_...  28.4 us
    gather x1, local copies, waits for them, and re-layouts, on_device(): found_rows = jnp.take(table_flat, jnp.maximum(asked_rows, 0), axis=0)  27.6 us
  transfers between devices with their start and end apart: 4, of which 3 were waited for; matrix products, arithmetic and copies ran while one was open for 12% of the time, Pallas kernels for 0%

commit v1 on v0

--- a/solution.py
+++ b/solution.py
@@ -142,7 +142,9 @@
         dense_grad.astype(jnp.bfloat16), "dp", scatter_dimension=1, tiled=True
     ).astype(jnp.float32)
     table_grad = table_grad.reshape(3, rows_dev, quarter)
-    totals = lax.psum((first_weights, second_weights, first_gains, second_gains), ("dp", "table"))
+    totals = lax.psum(
+        lax.psum((first_weights, second_weights, first_gains, second_gains), "table"), "dp"
+    )
     return (
         block_out,
         totals[0] * scale,

time: 690 us -> 819 us (1.19)
  waiting for transfers between devices: 256 us -> 328 us
  blocking collectives: 97.9 us -> 157 us
    psum x1 -> x2, waiting for transfers between devices: 33.9 us -> 217 us  [the longest x1 217 us: on_device(): lax.psum((first_weights, second_weights, first_gains, second_gains), 'tab...]
    all_to_all x1, waiting for transfers between devices: 111 us -> 0.01 us  [to_owners(): lax.all_to_all(outgoing, 'table', split_axis=0, concat_axis=0, tiled=True)]
    psum x1 -> x2, blocking collectives: 76.3 us -> 135 us  [the longest x1 127 us: on_device(): lax.psum((first_weights, second_weights, first_gains, second_gains), 'tab...]
  transfers between devices with their start and end apart: 4 -> 5, of which waited for: 3 -> 2; matrix products, arithmetic and copies ran while one was open for 12% -> 10% of each run, Pallas kernels for 0% -> 0%
where the time goes in v1:
time: 819 us; the launch traced here: 807 us
  waiting for transfers between devices  328 us (40%)
  blocking collectives  157 us (19%)
  other arithmetic  146 us (18%)
  local copies, waits for them, and re-layouts  140 us (17%)
  between operations  14.5 us (2%)
  starting transfers between devices  12.7 us (2%)
  matrix products  8.91 us (1%)
    psum x1, waiting for transfers between devices, on_device(): lax.psum((first_weights, second_weights, first_gains, second_gains), 'tab...  217 us
    psum x1, blocking collectives, on_device(): lax.psum((first_weights, second_weights, first_gains, second_gains), 'tab...  127 us
    all_to_all x1, waiting for transfers between devices, on_device(): lax.all_to_all(found_rows, 'table', split_axis=0, concat_axis=0, tiled=True)  111 us
    scatter-add x1, other arithmetic, on_device(): dense_grad = jnp.zeros((3 * rows_dev, width), jnp.float32).at[jnp.maximum...  64.8 us
    another operation x3, other arithmetic  37.3 us
    scatter x1, local copies, waits for them, and re-layouts, to_owners(): outgoing = jnp.zeros((shards * slot_count, width), jnp.bfloat16).at[slot_...  28.3 us
    gather x1, local copies, waits for them, and re-layouts, on_device(): found_rows = jnp.take(table_flat, jnp.maximum(asked_rows, 0), axis=0)  27.6 us
    scatter x1, local copies, waits for them, and re-layouts, on_device(): requests = jnp.full((shards * slot_count,), -1, jnp.int32).at[slot_place]...  22.8 us
  transfers between devices with their start and end apart: 5, of which 2 were waited for; matrix products, arithmetic and copies ran while one was open for 10% of the time, Pallas kernels for 0%

profile of v1, /device:TPU:2, one launch (start us, length us, event | category | flops | bytes accessed | tf_op | source)
XLA Modules:
  0.0 807.3 jit_solution(11630807067674048858)
XLA Ops:
  8.1 2.0 copy.48
  10.1 0.9 iota_multiply_fusion
  11.0 1.2 copy.53
  12.2 1.7 mul.226
  14.0 1.2 copy.54
  15.2 1.6 reshape.223
  16.8 1.6 reshape.220
  18.5 1.6 mul.229
  20.2 1.1 pad.33
  21.3 2.4 reshape.221
  23.7 35.5 %reduce-window.6 = s32[64,38,128]{2,1,0:T(8,128)} reduce-window(s32[64,38,128]{2,1,0:T(8,128)} %reshape.221, s32[]{:T(128)} %constant.37.clone.1), window={size=1x1x128 pad=0_0x0_0x127_0}, to_apply=%region_0.0 | reduce-window | flops 39534592 | bytes 2490372 | tf_op jit(solution)/shard_map/reduce-window
  59.2 2.8 slice.72
  62.0 1.9 copy.59
  64.1 1.6 broadcast_add_fusion
  66.2 22.8 %scatter_custom_fusion = s32[9728]{0:T(1024)S(1)} fusion(s32[4800]{0:T(1024)S(1)} %fusion.30, s32[4800]{0:T(1024)S(1)} %add.153, s32[]{:T(128)} %constant.40.clone.1), kind=kCustom, calls=%fused_computation.82 | custom fusion | bytes 38916 | tf_op jit(solution)/shard_map/scatter | solution.py:101
  89.3 21.6 %all_to_all.19 = s32[64,1,152]{2,1,0:T(1,128)S(1)} all-to-all(s32[64,1,152]{2,1,0:T(1,128)S(1)} %all_to_all.12), channel_id=1, replica_groups=mesh['dp'=4,'table'=64] {'table'}, dimensions={0} | all-to-all | bytes 77824 | tf_op jit(solution)/shard_map/all_to_all | solution.py:105
  111.0 27.6 %gather_fusion = bf16[9728,256]{1,0:T(8,128)(2,1)} fusion(bf16[6144,256]{1,0:T(8,128)(2,1)S(1)} %bitcast.55, s32[10240]{0:T(1024)S(1)} %pad_clamp_fusion), kind=kCustom, calls=%fused_computation | custom fusion | bytes 10000384 | tf_op jit(solution)/shard_map/jit(_take)/gather | solution.py:106
  138.7 8.1 %select_select_fusion = bf16[64,152,256]{2,1,0:T(8,128)(2,1)} fusion(bf16[64,152,256]{2,1,0:T(8,128)(2,1)} %bitcast.61, pred[64,152]{1,0:T(8,128)(4,1)S(1)} %get-tuple-element.61, pred[64,152]{1,0:T(8,128)(4,1)S(1)} %get-tuple-element.60), kind=kLoop, calls=%fused_computation.7 | loop fusion | flops 4980736 | bytes 9980928 | tf_op jit(solution)/shard_map/jit(_where)/select_n | solution.py:107
  146.8 6.2 all-to-all-start.1
  154.5 110.9 %all-to-all-done.1 = bf16[64,152,256]{2,1,0:T(8,128)(2,1)} async-done(((bf16[64,152,256]{2,1,0:T(8,128)(2,1)}), bf16[64,152,256]{2,1,0:T(8,128)(2,1)}, u32[]{:S(2)}, u32[]{:S(2)}) %all-to-all-start.1) | async-done | bytes 4980768 | tf_op jit(solution)/shard_map/all_to_all | solution.py:108
  265.4 13.8 %gather_fusion.1 = bf16[4800,256]{1,0:T(8,128)(2,1)S(1)} fusion(bf16[9728,256]{1,0:T(8,128)(2,1)} %bitcast.6, s32[5120]{0:T(1024)S(1)} %pad_clamp_fusion.1), kind=kCustom, calls=%fused_computation.1 | custom fusion | bytes 4934400 | tf_op jit(solution)/shard_map/jit(_take)/gather | solution.py:109
  279.2 3.8 gather.12
  283.0 13.2 %select_reduce_fusion = bf16[1600,256]{1,0:T(8,128)(2,1)S(1)} fusion(bf16[1600,3,256]{2,1,0:T(4,128)(2,1)} %gather.12, pred[1600,3]{1,0:T(8,128)(4,1)S(1)} %copy.52), kind=kLoop, calls=%fused_computation.8 | loop fusion | flops 2048000 | bytes 3281600 | tf_op jit(solution)/shard_map/reduce_sum | solution.py:113
  297.2 0.9 fusion.37
  298.8 1.1 multiply_convert_fusion.2
  301.2 0.9 fusion.38
  303.3 1.5 convert_multiply_fusion
  304.8 1.0 multiply_reduce_fusion
  305.8 2.4 multiply_convert_fusion.1
  309.8 1.7 fusion.20
  311.5 1.0 multiply_reduce_fusion.1
  312.5 1.3 multiply_convert_fusion
  315.5 7.5 broadcast_in_dim.70
  323.0 7.2 reshape.269
  330.2 28.3 %scatter_custom_fusion.1 = bf16[9728,256]{1,0:T(8,128)(2,1)} fusion(s32[4800]{0:T(1024)S(1)} %fusion.30, bf16[4800,256]{1,0:T(8,128)(2,1)} %reshape.269, bf16[]{:T(256)} %constant.72.clone.1), kind=kCustom, calls=%fused_computation.10 | custom fusion | bytes 4981248 | tf_op jit(solution)/shard_map/scatter | solution.py:76
  358.5 6.4 all-to-all-start.2
  365.0 3.6 fusion.24
  368.6 1.8 fusion.26
  370.5 216.7 %all-reduce.16.cloned.1.call-done = (f32[768,256]{1,0:T(8,128)}, f32[768,256]{1,0:T(8,128)}) async-done(((f32[768,256]{1,0:T(8,128)}, f32[768,256]{1,0:T(8,128)}), (f32[768,256]{1,0:T(8,128)}, f32[768,256]{1,0:T(8,128)})) %all-reduce.16.cloned.1.call-update) | async-done | bytes 1572880 | tf_op jit(solution)/shard_map/psum | solution.py:146
  587.2 64.8 %scatter_custom_fusion.2 = f32[6144,256]{1,0:T(8,128)} fusion(s32[9728]{0:T(1024)S(1)} %reshape.243, bf16[9728,256]{1,0:T(8,128)(2,1)} %bitcast.24, f32[]{:T(128)} %constant.73.clone.1), kind=kCustom, calls=%fused_computation.5 | custom fusion | flops 4980736 | bytes 11272196 | tf_op jit(solution)/shard_map/scatter-add | solution.py:139
  652.0 3.1 convert_element_type.64
  655.1 3.1 copy.60
  658.2 127.0 %all-reduce.9 = (f32[256]{0:T(256)S(1)}, f32[256]{0:T(256)S(1)}) all-reduce(f32[256]{0:T(256)S(1)} %get-tuple-element.38, f32[256]{0:T(256)S(1)} %get-tuple-element.36), channel_id=1, replica_groups=mesh['dp'=4,'table'=64] {'table'}, use_global_device_ids=true, to_apply=%region_18.19 | all-reduce | flops 512 | bytes 4096 | tf_op jit(solution)/shard_map/psum | solution.py:146
  785.2 8.4 %all-reduce.11 = (f32[256]{0:T(256)S(1)}, f32[256]{0:T(256)S(1)}) all-reduce(f32[256]{0:T(256)S(1)} %get-tuple-element.42, f32[256]{0:T(256)S(1)} %get-tuple-element.43), channel_id=1, replica_groups=mesh['dp'=4,'table'=64] {'dp'}, use_global_device_ids=true, to_apply=%region_19.20 | all-reduce | flops 512 | bytes 4096 | tf_op jit(solution)/shard_map/psum | solution.py:145
  794.8 2.2 broadcast_multiply_fusion.1
  797.0 1.0 broadcast_multiply_fusion
  797.9 1.4 bitcast_convert_fusion
  799.3 1.2 copy.70
  (87 shorter events, 12.2 us)
Async XLA Ops:
  7.2 103.8 %copy-start = (bf16[3,2048,256]{2,1,0:T(8,128)(2,1)S(1)}, bf16[3,2048,256]{2,1,0:T(8,128)(2,1)}, u32[]{:S(2)}) copy-start(bf16[3,2048,256]{2,1,0:T(8,128)(2,1)} %param.10) | copy-start | bytes 9437188
  8.1 5.9 copy-start.17
  146.8 118.6 %all-to-all-start.1 = ((bf16[64,152,256]{2,1,0:T(8,128)(2,1)}), bf16[64,152,256]{2,1,0:T(8,128)(2,1)}, u32[]{:S(2)}, u32[]{:S(2)}) async-start(bf16[64,152,256]{2,1,0:T(8,128)(2,1)} %select_select_fusion), calls=%async_computation.1 | async-start | bytes 9961472 | tf_op jit(solution)/shard_map/all_to_all | solution.py:108
  296.2 1.0 copy-start.16
  296.6 1.6 copy-start.8
  296.6 1.6 copy-start.10
  298.1 0.7 copy-start.18
  299.9 2.2 copy-start.6
  300.0 1.3 copy-start.15
  300.3 1.8 copy-start.12
  300.3 1.8 copy-start.13
  302.2 1.1 copy-start.7
  302.2 1.1 copy-start.19
  308.2 0.9 copy-start.2
  313.8 0.9 copy-start.4
  358.5 6.5 copy-start.3
  358.5 228.7 %all-to-all-start.2 = ((bf16[64,152,256]{2,1,0:T(8,128)(2,1)}), bf16[64,152,256]{2,1,0:T(8,128)(2,1)}, u32[]{:S(2)}, u32[]{:S(2)}) async-start(bf16[64,152,256]{2,1,0:T(8,128)(2,1)} %bitcast.60), calls=%async_computation.2 | async-start | bytes 9961472 | tf_op jit(solution)/shard_map/all_to_all | solution.py:79
  364.9 3.7 copy-start.5
  364.9 222.2 %all-reduce.16.cloned.1.call-start = ((), (), s32[]{:S(2)}) async-start(), calls=%async_computation.5 | async-start | bytes 3145728 | tf_op jit(solution)/shard_map/psum | solution.py:146
  365.0 3.6 copy-start.9
  365.0 3.6 copy-start.11
  370.5 424.4 %all-reduce.18.cloned.1.call-start = ((), (), s32[]{:S(2)}) async-start(), calls=%async_computation.6 | async-start | bytes 3145728 | tf_op jit(solution)/shard_map/psum | solution.py:145
  587.2 210.7 %reduce-scatter.4.cloned.1.call-start = ((), (), s32[]{:S(2)}) async-start(), calls=%async_computation.4 | async-start | bytes 3932160
  794.8 2.2 copy-start.14
  797.9 2.6 copy-start.1
Sparse Core Ops, SparseCore 0:
  370.6 216.5 all-reduce.15
  589.5 53.3 all-reduce.17
  658.3 36.4 reduce-scatter.3
